TPU v7x, 32 devices: a whole 2x2x4 slice. The times are simulated.
32 devices in a mesh: occ: 4 (over z), va: 2 (over x), vb: 4 (over y, core).
Axes of the slice: x: 2, y: 2, z: 4, core: 2. Of those that a mesh axis runs over, the one named last changes fastest.
Arguments:
- aux_factors: bfloat16 [4, 1024, 2048], P('occ', ('vb', 'va')), may hold values from -0.59765625 to 0.59765625
- occ_energy: float32 [4], replicated, may hold values from -2 to -0.5
- vir_energy: float32 [1024], replicated, may hold values from 0.5 to 3
- occ_index: int32 [4], replicated, may hold values from 0 to 3, each once
- vir_index: int32 [1024], replicated, may hold values from 0 to 1023, each once
Outputs:
- gamma_aux: float32 [4, 1024, 2048], P('occ', ('vb', 'va'))
Inputs may be any that keep to these rules, and one draw needn't show every extreme that they name: `occ_index`: each occupied table row appears exactly once. `vir_index`: each virtual table row appears exactly once.
All inputs are finite; a program needn't handle non-finite values.
Results may differ from a plain program's by a relative error of at most 0.0017.
Values may be sent and summed in bfloat16 or wider, within the bound.
No kernel may reach another device: no remote copies, remote signals or barrier semaphores. Data moves between devices by JAX's collectives and lax.ppermute only.
A program may use at most 64 MiB of HBM per device.

v0:
```python
import jax
import jax.numpy as jnp
from jax import lax
from jax.sharding import PartitionSpec as P

STEPS = 4


def passed_along(block, axis, distance):
    devices = range(lax.axis_size(axis))
    route = [((i - distance) % len(devices), i) for i in devices]
    return lax.ppermute(block, axis, route)


def lookup(indices, energies):
    positions = jnp.arange(energies.shape[0], dtype=jnp.int32)
    matches = indices[:, None] == positions[None, :]
    return jnp.sum(jnp.where(matches, energies[None, :], 0.0), axis=1)


def per_device(aux_factors, occ_energy, vir_energy, occ_index, vir_index):
    va_count = lax.axis_size("va")
    vb_count = lax.axis_size("vb")
    occ_count = lax.axis_size("occ")
    va_rank = lax.axis_index("va")
    vb_rank = lax.axis_index("vb")
    occ_rank = lax.axis_index("occ")
    occ_rows, block_width, aux_width = aux_factors.shape
    vir_width = vir_index.shape[0]
    row_count = vb_count * block_width
    col_count = va_count * block_width
    row_index = lax.dynamic_index_in_dim(
        vir_index.reshape(vb_count, va_count, block_width), va_rank, 1, False
    ).reshape(row_count)
    col_index = lax.dynamic_index_in_dim(
        vir_index.reshape(vb_count, vir_width // vb_count), vb_rank, 0, False
    )
    row_energy = lookup(row_index, vir_energy)
    col_energy = lookup(col_index, vir_energy)

    def block_energy(block_id):
        return lookup(
            lax.dynamic_slice_in_dim(occ_index, block_id * occ_rows, occ_rows), occ_energy
        )

    own_energy = block_energy(occ_rank)
    own_columns = lax.all_gather(aux_factors, "va", axis=1, tiled=True)
    own_rows = lax.all_gather(aux_factors, "vb", axis=1, tiled=True)
    gradient = jnp.zeros((occ_rows, row_count, aux_width), jnp.float32)
    far_columns = own_columns
    for distance in range(STEPS):
        if distance > 0:
            far_columns = passed_along(far_columns, "occ", 1)
        far_block = (occ_rank - distance + occ_count) % occ_count
        kernel = jnp.einsum(
            "iap,jbp->iajb", own_rows, far_columns, preferred_element_type=jnp.float32
        )
        outgoing = kernel.reshape(occ_rows, vb_count, block_width, occ_rows, va_count, block_width)
        outgoing = outgoing.transpose(4, 1, 0, 2, 3, 5).reshape(
            va_count * vb_count, occ_rows, block_width, occ_rows, block_width
        )
        incoming = lax.all_to_all(outgoing, ("va", "vb"), split_axis=0, concat_axis=0, tiled=True)
        incoming = incoming.reshape(
            va_count, vb_count, occ_rows, block_width, occ_rows, block_width
        )
        swapped = incoming.transpose(2, 1, 5, 4, 0, 3).reshape(
            occ_rows, row_count, occ_rows, col_count
        )
        energy_gap = (
            own_energy[:, None, None, None]
            + block_energy(far_block)[None, None, :, None]
            - row_energy[None, :, None, None]
            - col_energy[None, None, None, :]
        )
        weights = ((2.0 * kernel - swapped) / energy_gap).astype(jnp.bfloat16)
        gradient = gradient + jnp.einsum(
            "iajb,jbp->iap", weights, far_columns, preferred_element_type=jnp.float32
        )
    return lax.psum_scatter(gradient, "vb", scatter_dimension=1, tiled=True)


def solution(mesh):
    return jax.shard_map(
        per_device,
        mesh=mesh,
        in_specs=(P("occ", ("vb", "va"), None), P(), P(), P(), P()),
        out_specs=P("occ", ("vb", "va"), None),
        check_vma=False,
    )
```

profile of v0, /device:TPU:0, one launch (start us, length us, event | category | flops | bytes accessed | tf_op | source)
XLA Modules:
  0.0 195.6 jit_solution(13095508665357366006)
XLA Ops:
  6.5 0.7 all-gather.5.cloned.1.call-update
  7.3 0.0 all-gather.3.cloned.1.call-start
  7.3 0.7 all-gather.3.cloned.1.call-update
  8.0 24.9 %all-gather.5.cloned.1.call-done = bf16[1,256,2048]{2,1,0:T(8,128)(2,1)} async-done(((bf16[1,128,2048]{2,1,0:T(8,128)(2,1)}), bf16[1,256,2048]{2,1,0:T(8,128)(2,1)}) %all-gather.5.cloned.1.call-update) | async-done | bytes 1048592 | tf_op jit(solution)/shard_map/all_gather | solution.py:47
  32.9 1.5 collective-permute-start
  34.4 25.3 %collective-permute-done = bf16[1,256,2048]{2,1,0:T(8,128)(2,1)S(1)} collective-permute-done((bf16[1,256,2048]{2,1,0:T(8,128)(2,1)}, bf16[1,256,2048]{2,1,0:T(8,128)(2,1)S(1)}, u32[]{:S(2)}, u32[]{:S(2)}) %collective-permute-start) | collective-permute-done | bytes 1048608 | tf_op jit(solution)/shard_map/ppermute | solution.py:12
  59.7 0.0 collective-permute-start.1
  59.7 1.6 fusion.52
  61.2 4.4 %fusion.47 = (f32[]{:T(128)}, f32[]{:T(128)}, f32[]{:T(128)}, f32[]{:T(128)}, f32[]{:T(128)}) fusion(f32[4]{0:T(128)} %param.6, s32[]{:T(128)} %bitcast.32, s32[]{:T(128)} %bitcast.18, s32[]{:T(128)} %bitcast.8, s32[]{:T(128)} %bitcast.7, s32[]{:T(128)} %bitcast.25), kind=kLoop, calls=%fused_computation.61 | loop fusion | flops 55 | bytes 56 | tf_op jit(solution)/shard_map/reduce_sum | solution.py:18
  70.6 0.7 reshape.218
  71.3 0.7 constant_dynamic-slice_fusion.1
  72.0 1.0 select_reduce_fusion
  73.1 12.3 %collective-permute-done.1 = bf16[1,256,2048]{2,1,0:T(8,128)(2,1)S(1)} collective-permute-done((bf16[1,256,2048]{2,1,0:T(8,128)(2,1)S(1)}, bf16[1,256,2048]{2,1,0:T(8,128)(2,1)S(1)}, u32[]{:S(2)}, u32[]{:S(2)}) %collective-permute-start.1) | collective-permute-done | bytes 1048608 | tf_op jit(solution)/shard_map/ppermute | solution.py:12
  85.3 2.7 %fusion.2 = f32[512,256]{1,0:T(8,128)S(1)} fusion(bf16[1,512,2048]{2,1,0:T(8,128)(2,1)} %all-gather.3.cloned.1.call-done, bf16[1,256,2048]{2,1,0:T(8,128)(2,1)S(1)} %collective-permute-done.1), kind=kOutput, calls=%fused_computation.3 | convolution fusion | flops 536870912 | bytes 3670016 | tf_op jit(solution)/shard_map/iap,jbp->iajb/dot_general | solution.py:55
  88.1 0.3 reshape.225
  88.3 0.8 copy.32
  89.2 3.5 %all-to-all-start.2 = ((f32[8,1,128,1,128]{4,2,3,1,0:T(8,128)}), f32[8,1,128,1,128]{4,2,3,1,0:T(8,128)S(1)}, u32[]{:S(2)}, u32[]{:S(2)}) async-start(f32[8,1,128,1,128]{4,2,3,1,0:T(8,128)} %bitcast.22), calls=%async_computation.2 | async-start | bytes 1048576 | tf_op jit(solution)/shard_map/all_to_all | solution.py:62
  92.7 0.1 collective-permute-start.2
  92.8 2.3 %fusion.4 = f32[512,256]{1,0:T(8,128)S(1)} fusion(bf16[1,512,2048]{2,1,0:T(8,128)(2,1)} %all-gather.3.cloned.1.call-done, bf16[1,256,2048]{2,1,0:T(8,128)(2,1)S(1)} %collective-permute-done), kind=kOutput, calls=%fused_computation.5 | convolution fusion | flops 536870912 | bytes 3670016 | tf_op jit(solution)/shard_map/iap,jbp->iajb/dot_general | solution.py:55
  95.1 0.0 copy-start.2
  95.1 0.3 reshape.220
  95.4 0.8 copy.29
  96.2 5.2 %all-to-all-done.2 = f32[8,1,128,1,128]{4,2,3,1,0:T(8,128)S(1)} async-done(((f32[8,1,128,1,128]{4,2,3,1,0:T(8,128)}), f32[8,1,128,1,128]{4,2,3,1,0:T(8,128)S(1)}, u32[]{:S(2)}, u32[]{:S(2)}) %all-to-all-start.2) | async-done | bytes 524320 | tf_op jit(solution)/shard_map/all_to_all | solution.py:62
  101.5 3.5 %all-to-all-start.1 = ((f32[8,1,128,1,128]{4,2,3,1,0:T(8,128)}), f32[8,1,128,1,128]{4,2,3,1,0:T(8,128)S(1)}, u32[]{:S(2)}, u32[]{:S(2)}) async-start(f32[8,1,128,1,128]{4,2,3,1,0:T(8,128)} %bitcast.15), calls=%async_computation.1 | async-start | bytes 1048576 | tf_op jit(solution)/shard_map/all_to_all | solution.py:62
  105.0 0.2 select_reduce_fusion.1
  105.2 2.6 %fusion.6 = f32[512,256]{1,0:T(8,128)S(1)} fusion(bf16[1,512,2048]{2,1,0:T(8,128)(2,1)} %all-gather.3.cloned.1.call-done, bf16[1,256,2048]{2,1,0:T(8,128)(2,1)} %all-gather.5.cloned.1.call-done), kind=kOutput, calls=%fused_computation.7 | convolution fusion | flops 536870912 | bytes 3670016 | tf_op jit(solution)/shard_map/iap,jbp->iajb/dot_general | solution.py:55
  107.8 0.3 reshape.213
  108.1 0.8 copy.26
  109.0 0.3 copy.34
  109.2 4.5 %all-to-all-done.1 = f32[8,1,128,1,128]{4,2,3,1,0:T(8,128)S(1)} async-done(((f32[8,1,128,1,128]{4,2,3,1,0:T(8,128)}), f32[8,1,128,1,128]{4,2,3,1,0:T(8,128)S(1)}, u32[]{:S(2)}, u32[]{:S(2)}) %all-to-all-start.1) | async-done | bytes 524320 | tf_op jit(solution)/shard_map/all_to_all | solution.py:62
  113.7 3.5 %all-to-all-start = ((f32[8,1,128,1,128]{4,2,3,1,0:T(8,128)}), f32[8,1,128,1,128]{4,2,3,1,0:T(8,128)S(1)}, u32[]{:S(2)}, u32[]{:S(2)}) async-start(f32[8,1,128,1,128]{4,2,3,1,0:T(8,128)} %bitcast.118), calls=%async_computation | async-start | bytes 1048576 | tf_op jit(solution)/shard_map/all_to_all | solution.py:62
  117.2 3.9 %fusion.10 = f32[512,2048]{1,0:T(8,128)} fusion(bf16[1,256,2048]{2,1,0:T(8,128)(2,1)} %copy-done.1, f32[64,8,2,128]{3,2,1,0:T(2,128)S(1)} %bitcast.112, f32[512,256]{1,0:T(8,128)S(1)} %fusion.2, f32[512]{0:T(512)S(1)} %get-tuple-element.11, f32[256]{0:T(256)S(1)} %select_reduce_fusion.1), kind=kOutput, calls=%fused_computation.13 | convolution fusion | flops 537526272 | bytes 6294528 | tf_op jit(solution)/shard_map/iajb,jbp->iap/dot_general | solution.py:76
  121.2 0.3 copy.31
  121.4 0.0 collective-permute-done.2
  121.4 2.6 %fusion = f32[512,256]{1,0:T(8,128)S(1)} fusion(bf16[1,512,2048]{2,1,0:T(8,128)(2,1)} %all-gather.3.cloned.1.call-done, bf16[1,256,2048]{2,1,0:T(8,128)(2,1)} %collective-permute-done.2), kind=kOutput, calls=%fused_computation.1 | convolution fusion | flops 536870912 | bytes 3670016 | tf_op jit(solution)/shard_map/iap,jbp->iajb/dot_general | solution.py:55
  124.0 0.3 reshape.230
  124.3 0.8 copy.35
  125.1 0.9 all-to-all-done
  126.0 3.5 %all-to-all-start.3 = ((f32[8,1,128,1,128]{4,2,3,1,0:T(8,128)}), f32[8,1,128,1,128]{4,2,3,1,0:T(8,128)S(1)}, u32[]{:S(2)}, u32[]{:S(2)}) async-start(f32[8,1,128,1,128]{4,2,3,1,0:T(8,128)} %bitcast.29), calls=%async_computation.3 | async-start | bytes 1048576 | tf_op jit(solution)/shard_map/all_to_all | solution.py:62
  129.5 0.0 reduce-scatter.2.cloned.1.call-start
  129.6 4.0 %fusion.13 = f32[512,2048]{1,0:T(8,128)} fusion(bf16[1,256,2048]{2,1,0:T(8,128)(2,1)} %copy-done, f32[64,8,2,128]{3,2,1,0:T(2,128)S(1)} %bitcast.111, f32[512,256]{1,0:T(8,128)S(1)} %fusion.4, f32[512]{0:T(512)S(1)} %get-tuple-element.12, f32[256]{0:T(256)S(1)} %select_reduce_fusion.1), kind=kOutput, calls=%fused_computation.16 | convolution fusion | flops 537526272 | bytes 6294528 | tf_op jit(solution)/shard_map/iajb,jbp->iap/dot_general | solution.py:76
  133.6 0.3 copy.28
  133.8 4.0 %fusion.16 = f32[512,2048]{1,0:T(8,128)} fusion(bf16[1,256,2048]{2,1,0:T(8,128)(2,1)} %all-gather.5.cloned.1.call-done, f32[64,8,2,128]{3,2,1,0:T(2,128)S(1)} %bitcast.114, f32[512,256]{1,0:T(8,128)S(1)} %fusion.6, f32[256]{0:T(256)S(1)} %select_reduce_fusion.1, f32[512]{0:T(512)S(1)} %get-tuple-element.13), kind=kOutput, calls=%fused_computation.19 | convolution fusion | flops 537526272 | bytes 6294528 | tf_op jit(solution)/shard_map/iajb,jbp->iap/dot_general | solution.py:76
  137.8 0.5 all-to-all-done.3
  138.3 0.3 copy.37
  138.6 7.8 %add_bitcast_fusion = f32[1,512,2048]{2,1,0:T(8,128)} fusion(f32[512,2048]{1,0:T(8,128)} %fusion.10, f32[512,2048]{1,0:T(8,128)} %fusion.16, f32[512,2048]{1,0:T(8,128)} %fusion.13, bf16[1,256,2048]{2,1,0:T(8,128)(2,1)} %collective-permute-done.2, f32[64,8,2,128]{3,2,1,0:T(2,128)S(1)} %bitcast.113, f32[512,256]{1,0:T(8,128)S(1)} %fusion, ...), kind=kOutput, calls=%fused_computation | convolution fusion | flops 540672000 | bytes 18877440 | tf_op jit(solution)/shard_map/iajb,jbp->iap/dot_general | solution.py:76
  146.3 0.0 reduce-scatter.2.cloned.1.call-update
  146.4 42.8 %reduce-scatter.2.cloned.1.call-done = f32[1,128,2048]{2,1,0:T(8,128)} async-done(((f32[1,512,2048]{2,1,0:T(8,128)}), f32[1,128,2048]{2,1,0:T(8,128)}) %reduce-scatter.2.cloned.1.call-update) | async-done | bytes 1048592 | tf_op jit(solution)/shard_map/reduce_scatter | solution.py:79
  (9 shorter events, 0.0 us)
Async XLA Ops:
  6.5 26.4 %all-gather.5.cloned.1.call-start = ((), (), s32[]{:S(2)}) async-start(), calls=%async_computation.6 | async-start | bytes 1572864 | tf_op jit(solution)/shard_map/all_gather | solution.py:47
  7.3 78.1 %all-gather.3.cloned.1.call-start = ((), (), s32[]{:S(2)}) async-start(), calls=%async_computation.5 | async-start | bytes 2621440 | tf_op jit(solution)/shard_map/all_gather | solution.py:48
  32.9 26.7 %collective-permute-start = (bf16[1,256,2048]{2,1,0:T(8,128)(2,1)}, bf16[1,256,2048]{2,1,0:T(8,128)(2,1)S(1)}, u32[]{:S(2)}, u32[]{:S(2)}) collective-permute-start(bf16[1,256,2048]{2,1,0:T(8,128)(2,1)} %all-gather.5.cloned.1.call-done), channel_id=1, source_target_pairs={{24,0},{0,8},{8,16},{16,24},{25,1},{1,9},{9,17},{17,25},{26,2},{2,... | collective-permute-start | bytes 3145736 | tf_op jit(solution)/shard_map/ppermute | solution.py:12
  59.7 33.1 %copy-start = (bf16[1,256,2048]{2,1,0:T(8,128)(2,1)}, bf16[1,256,2048]{2,1,0:T(8,128)(2,1)S(1)}, u32[]{:S(2)}) copy-start(bf16[1,256,2048]{2,1,0:T(8,128)(2,1)S(1)} %collective-permute-done) | copy-start | bytes 3145732
  59.7 25.7 %collective-permute-start.1 = (bf16[1,256,2048]{2,1,0:T(8,128)(2,1)S(1)}, bf16[1,256,2048]{2,1,0:T(8,128)(2,1)S(1)}, u32[]{:S(2)}, u32[]{:S(2)}) collective-permute-start(bf16[1,256,2048]{2,1,0:T(8,128)(2,1)S(1)} %collective-permute-done), channel_id=1, source_target_pairs={{24,0},{0,8},{8,16},{16,24},{25,1},{1,9},{9,17},{17,25},{26,2},{2,... | collective-permute-start | bytes 3145736 | tf_op jit(solution)/shard_map/ppermute | solution.py:12
  85.3 2.7 %copy-start.1 = (bf16[1,256,2048]{2,1,0:T(8,128)(2,1)}, bf16[1,256,2048]{2,1,0:T(8,128)(2,1)S(1)}, u32[]{:S(2)}) copy-start(bf16[1,256,2048]{2,1,0:T(8,128)(2,1)S(1)} %collective-permute-done.1) | copy-start | bytes 3145732
  89.2 12.3 %all-to-all-start.2 = ((f32[8,1,128,1,128]{4,2,3,1,0:T(8,128)}), f32[8,1,128,1,128]{4,2,3,1,0:T(8,128)S(1)}, u32[]{:S(2)}, u32[]{:S(2)}) async-start(f32[8,1,128,1,128]{4,2,3,1,0:T(8,128)} %bitcast.22), calls=%async_computation.2 | async-start | bytes 1048576 | tf_op jit(solution)/shard_map/all_to_all | solution.py:62
  92.7 28.7 %collective-permute-start.2 = (bf16[1,256,2048]{2,1,0:T(8,128)(2,1)}, bf16[1,256,2048]{2,1,0:T(8,128)(2,1)}, u32[]{:S(2)}, u32[]{:S(2)}) collective-permute-start(bf16[1,256,2048]{2,1,0:T(8,128)(2,1)} %copy-done.1), channel_id=1, source_target_pairs={{24,0},{0,8},{8,16},{16,24},{25,1},{1,9},{9,17},{17,25},{26,2},{2,... | collective-permute-start | bytes 3145736 | tf_op jit(solution)/shard_map/ppermute | solution.py:12
  95.1 9.9 %copy-start.2 = (f32[1024]{0:T(1024)S(1)}, f32[1024]{0:T(1024)}, u32[]{:S(2)}) copy-start(f32[1024]{0:T(1024)} %param.7) | copy-start | bytes 12292
  101.5 12.3 %all-to-all-start.1 = ((f32[8,1,128,1,128]{4,2,3,1,0:T(8,128)}), f32[8,1,128,1,128]{4,2,3,1,0:T(8,128)S(1)}, u32[]{:S(2)}, u32[]{:S(2)}) async-start(f32[8,1,128,1,128]{4,2,3,1,0:T(8,128)} %bitcast.15), calls=%async_computation.1 | async-start | bytes 1048576 | tf_op jit(solution)/shard_map/all_to_all | solution.py:62
  113.7 12.3 %all-to-all-start = ((f32[8,1,128,1,128]{4,2,3,1,0:T(8,128)}), f32[8,1,128,1,128]{4,2,3,1,0:T(8,128)S(1)}, u32[]{:S(2)}, u32[]{:S(2)}) async-start(f32[8,1,128,1,128]{4,2,3,1,0:T(8,128)} %bitcast.118), calls=%async_computation | async-start | bytes 1048576 | tf_op jit(solution)/shard_map/all_to_all | solution.py:62
  126.0 12.3 %all-to-all-start.3 = ((f32[8,1,128,1,128]{4,2,3,1,0:T(8,128)}), f32[8,1,128,1,128]{4,2,3,1,0:T(8,128)S(1)}, u32[]{:S(2)}, u32[]{:S(2)}) async-start(f32[8,1,128,1,128]{4,2,3,1,0:T(8,128)} %bitcast.29), calls=%async_computation.3 | async-start | bytes 1048576 | tf_op jit(solution)/shard_map/all_to_all | solution.py:62
  129.5 59.6 %reduce-scatter.2.cloned.1.call-start = ((), (), s32[]{:S(2)}) async-start(), calls=%async_computation.7 | async-start | bytes 5242880 | tf_op jit(solution)/shard_map/reduce_scatter | solution.py:79
Sparse Core Ops, SparseCore 0:
  8.9 23.9 all-gather.4
  34.5 22.5 all-gather.2
  146.5 42.5 reduce-scatter.1
where the time goes:
time: 197 us; the launch traced here: 196 us
  waiting for transfers between devices  118 us (60%)
  matrix products  29.9 us (15%)
  between operations  18.3 us (9%)
  starting transfers between devices  15.6 us (8%)
  local copies, waits for them, and re-layouts  8.41 us (4%)
  other arithmetic  5.74 us (3%)
    reduce_scatter x1, waiting for transfers between devices, per_device(): return lax.psum_scatter(gradient, 'vb', scatter_dimension=1, tiled=True)  42.8 us
    ppermute x3, waiting for transfers between devices, passed_along(): return lax.ppermute(block, axis, route)  37.5 us
    all_gather x1, waiting for transfers between devices, per_device(): own_columns = lax.all_gather(aux_factors, 'va', axis=1, tiled=True)  24.9 us
    dot_general x4, matrix products, per_device(): jnp.einsum('iajb,jbp->iap', weights, far_columns, preferred_element_type=...  19.6 us
    all_to_all x4, starting transfers between devices, per_device(): lax.all_to_all(outgoing, ('va', 'vb'), split_axis=0, concat_axis=0, tiled...  14 us
    all_to_all x4, waiting for transfers between devices, per_device(): lax.all_to_all(outgoing, ('va', 'vb'), split_axis=0, concat_axis=0, tiled...  11.1 us
    dot_general x4, matrix products, per_device(): jnp.einsum('iap,jbp->iajb', own_rows, far_columns, preferred_element_type...  10.2 us
    reduce_sum x3, other arithmetic, lookup(): return jnp.sum(jnp.where(matches, energies[None, :], 0.0), axis=1)  5.73 us
  transfers between devices with their start and end apart: 10, of which 8 were waited for; matrix products, arithmetic and copies ran while one was open for 16% of the time, Pallas kernels for 0%

commit v1 on v0

--- a/solution.py
+++ b/solution.py
@@ -4,6 +4,12 @@
 from jax.sharding import PartitionSpec as P
 
 STEPS = 4
+
+
+def choose_sizes_on_mesh(row_data):
+    fresh = lax.all_gather(row_data, "va")
+    even = jnp.concatenate(fresh, axis=1)
+    return even
 
 
 def passed_along(block, axis, distance):
@@ -44,7 +50,7 @@
         )
 
     own_energy = block_energy(occ_rank)
-    own_columns = lax.all_gather(aux_factors, "va", axis=1, tiled=True)
+    own_columns = choose_sizes_on_mesh(aux_factors)
     own_rows = lax.all_gather(aux_factors, "vb", axis=1, tiled=True)
     gradient = jnp.zeros((occ_rows, row_count, aux_width), jnp.float32)
     far_columns = own_columns

time: 197 us -> 187 us (0.949)
  waiting for transfers between devices: 118 us -> 109 us
    all_to_all x4, waiting for transfers between devices: 11.1 us -> 5.03 us  [per_device(): lax.all_to_all(outgoing, ('va', 'vb'), split_axis=0, concat_axis=0, tiled...]
    ppermute x3, waiting for transfers between devices: 37.5 us -> 31.7 us  [passed_along(): return lax.ppermute(block, axis, route)]
    reduce_scatter x1, waiting for transfers between devices: 42.8 us -> 45.5 us  [per_device(): return lax.psum_scatter(gradient, 'vb', scatter_dimension=1, tiled=True)]
  transfers between devices with their start and end apart: 10 -> 10, of which waited for: 8 -> 7; matrix products, arithmetic and copies ran while one was open for 16% -> 19% of each run, Pallas kernels for 0% -> 0%
where the time goes in v1:
time: 187 us
  waiting for transfers between devices  109 us (58%)
  matrix products  30 us (16%)
  between operations  18.3 us (10%)
  starting transfers between devices  15.5 us (8%)
  local copies, waits for them, and re-layouts  8.51 us (5%)
  other arithmetic  5.68 us (3%)
    reduce_scatter x1, waiting for transfers between devices, per_device(): return lax.psum_scatter(gradient, 'vb', scatter_dimension=1, tiled=True)  45.5 us
    ppermute x3, waiting for transfers between devices, passed_along(): return lax.ppermute(block, axis, route)  31.7 us
    all_gather x1, waiting for transfers between devices, choose_sizes_on_mesh(): fresh = lax.all_gather(row_data, 'va')  24.9 us
    dot_general x4, matrix products, per_device(): jnp.einsum('iajb,jbp->iap', weights, far_columns, preferred_element_type=...  19.6 us
    all_to_all x4, starting transfers between devices, per_device(): lax.all_to_all(outgoing, ('va', 'vb'), split_axis=0, concat_axis=0, tiled...  14 us
    dot_general x4, matrix products, per_device(): jnp.einsum('iap,jbp->iajb', own_rows, far_columns, preferred_element_type...  10.4 us
    reduce_sum x3, other arithmetic, lookup(): return jnp.sum(jnp.where(matches, energies[None, :], 0.0), axis=1)  5.67 us
    all_to_all x4, waiting for transfers between devices, per_device(): lax.all_to_all(outgoing, ('va', 'vb'), split_axis=0, concat_axis=0, tiled...  5.03 us
  transfers between devices with their start and end apart: 10, of which 7 were waited for; matrix products, arithmetic and copies ran while one was open for 19% of the time, Pallas kernels for 0%

profile of v1, /device:TPU:0, one launch (start us, length us, event | category | flops | bytes accessed | tf_op | source)
XLA Modules:
  0.0 186.7 jit_solution(12958665771549099180)
XLA Ops:
  6.5 0.7 all-gather.6.cloned.1.call-update
  7.3 0.0 all-gather.4.cloned.1.call-start
  7.3 0.7 all-gather.4.cloned.1.call-update
  8.0 24.9 %all-gather.6.cloned.1.call-done = bf16[2,128,2048]{2,1,0:T(8,128)(2,1)} async-done(((bf16[1,128,2048]{2,1,0:T(8,128)(2,1)}), bf16[2,128,2048]{2,1,0:T(8,128)(2,1)}) %all-gather.6.cloned.1.call-update) | async-done | bytes 1048592 | tf_op jit(solution)/shard_map/all_gather | solution.py:10
  32.9 1.5 collective-permute-start
  34.4 25.3 %collective-permute-done = bf16[1,256,2048]{2,1,0:T(8,128)(2,1)S(1)} collective-permute-done((bf16[1,256,2048]{2,1,0:T(8,128)(2,1)}, bf16[1,256,2048]{2,1,0:T(8,128)(2,1)S(1)}, u32[]{:S(2)}, u32[]{:S(2)}) %collective-permute-start) | collective-permute-done | bytes 1048608 | tf_op jit(solution)/shard_map/ppermute | solution.py:18
  59.7 0.0 collective-permute-start.1
  59.7 1.5 fusion.50
  61.2 4.4 %fusion.45 = (f32[]{:T(128)}, f32[]{:T(128)}, f32[]{:T(128)}, f32[]{:T(128)}, f32[]{:T(128)}) fusion(f32[4]{0:T(128)} %param.6, s32[]{:T(128)} %bitcast.33, s32[]{:T(128)} %bitcast.19, s32[]{:T(128)} %bitcast.8, s32[]{:T(128)} %bitcast.7, s32[]{:T(128)} %bitcast.26), kind=kLoop, calls=%fused_computation.59 | loop fusion | flops 55 | bytes 56 | tf_op jit(solution)/shard_map/reduce_sum | solution.py:24
  70.6 0.7 reshape.223
  71.3 0.7 constant_dynamic-slice_fusion.1
  72.0 1.0 select_reduce_fusion
  73.1 0.0 all-gather.4.cloned.1.call-done
  73.1 2.6 %fusion.6 = f32[512,256]{1,0:T(8,128)S(1)} fusion(bf16[256,2048]{1,0:T(8,128)(2,1)} %bitcast.120, bf16[1,512,2048]{2,1,0:T(8,128)(2,1)} %all-gather.4.cloned.1.call-done), kind=kOutput, calls=%fused_computation.7 | convolution fusion | flops 536870912 | bytes 3670016 | tf_op jit(solution)/shard_map/iap,jbp->iajb/dot_general | solution.py:61
  75.7 0.3 reshape.218
  76.0 0.9 copy.26
  76.9 3.5 %all-to-all-start = ((f32[8,1,128,1,128]{4,2,3,1,0:T(8,128)}), f32[8,1,128,1,128]{4,2,3,1,0:T(8,128)S(1)}, u32[]{:S(2)}, u32[]{:S(2)}) async-start(f32[8,1,128,1,128]{4,2,3,1,0:T(8,128)} %bitcast.4), calls=%async_computation | async-start | bytes 1048576 | tf_op jit(solution)/shard_map/all_to_all | solution.py:68
  80.4 5.0 %collective-permute-done.1 = bf16[1,256,2048]{2,1,0:T(8,128)(2,1)} collective-permute-done((bf16[1,256,2048]{2,1,0:T(8,128)(2,1)S(1)}, bf16[1,256,2048]{2,1,0:T(8,128)(2,1)}, u32[]{:S(2)}, u32[]{:S(2)}) %collective-permute-start.1) | collective-permute-done | bytes 1048608 | tf_op jit(solution)/shard_map/ppermute | solution.py:18
  85.4 0.0 collective-permute-start.2
  85.4 2.6 %fusion.2 = f32[512,256]{1,0:T(8,128)S(1)} fusion(bf16[1,512,2048]{2,1,0:T(8,128)(2,1)} %all-gather.4.cloned.1.call-done, bf16[1,256,2048]{2,1,0:T(8,128)(2,1)} %collective-permute-done.1), kind=kOutput, calls=%fused_computation.3 | convolution fusion | flops 536870912 | bytes 3670016 | tf_op jit(solution)/shard_map/iap,jbp->iajb/dot_general | solution.py:61
  88.0 0.0 copy-start.1
  88.0 0.3 reshape.231
  88.3 0.9 copy.32
  89.2 0.0 all-to-all-done
  89.2 3.5 %all-to-all-start.2 = ((f32[8,1,128,1,128]{4,2,3,1,0:T(8,128)}), f32[8,1,128,1,128]{4,2,3,1,0:T(8,128)S(1)}, u32[]{:S(2)}, u32[]{:S(2)}) async-start(f32[8,1,128,1,128]{4,2,3,1,0:T(8,128)} %bitcast.23), calls=%async_computation.2 | async-start | bytes 1048576 | tf_op jit(solution)/shard_map/all_to_all | solution.py:68
  92.7 0.2 select_reduce_fusion.1
  93.0 2.6 %fusion.4 = f32[512,256]{1,0:T(8,128)S(1)} fusion(bf16[1,512,2048]{2,1,0:T(8,128)(2,1)} %all-gather.4.cloned.1.call-done, bf16[1,256,2048]{2,1,0:T(8,128)(2,1)} %copy-done), kind=kOutput, calls=%fused_computation.5 | convolution fusion | flops 536870912 | bytes 3670016 | tf_op jit(solution)/shard_map/iap,jbp->iajb/dot_general | solution.py:61
  95.6 0.3 reshape.226
  95.9 0.9 copy.29
  96.8 0.3 copy.28
  97.0 4.5 %all-to-all-done.2 = f32[8,1,128,1,128]{4,2,3,1,0:T(8,128)S(1)} async-done(((f32[8,1,128,1,128]{4,2,3,1,0:T(8,128)}), f32[8,1,128,1,128]{4,2,3,1,0:T(8,128)S(1)}, u32[]{:S(2)}, u32[]{:S(2)}) %all-to-all-start.2) | async-done | bytes 524320 | tf_op jit(solution)/shard_map/all_to_all | solution.py:68
  101.5 3.5 %all-to-all-start.1 = ((f32[8,1,128,1,128]{4,2,3,1,0:T(8,128)}), f32[8,1,128,1,128]{4,2,3,1,0:T(8,128)S(1)}, u32[]{:S(2)}, u32[]{:S(2)}) async-start(f32[8,1,128,1,128]{4,2,3,1,0:T(8,128)} %bitcast.117), calls=%async_computation.1 | async-start | bytes 1048576 | tf_op jit(solution)/shard_map/all_to_all | solution.py:68
  105.0 3.9 %fusion.24 = f32[512,2048]{1,0:T(8,128)} fusion(bf16[256,2048]{1,0:T(8,128)(2,1)} %bitcast.121, f32[64,8,2,128]{3,2,1,0:T(2,128)S(1)} %bitcast.111, f32[512,256]{1,0:T(8,128)S(1)} %fusion.6, f32[256]{0:T(256)S(1)} %select_reduce_fusion.1, f32[512]{0:T(512)S(1)} %get-tuple-element.13), kind=kOutput, calls=%fused_computation.33 | convolution fusion | flops 537526272 | bytes 6294528 | tf_op jit(solution)/shard_map/iajb,jbp->iap/dot_general | solution.py:82
  108.9 0.3 copy.34
  109.2 1.4 collective-permute-done.2
  110.6 2.6 %fusion = f32[512,256]{1,0:T(8,128)S(1)} fusion(bf16[1,512,2048]{2,1,0:T(8,128)(2,1)} %all-gather.4.cloned.1.call-done, bf16[1,256,2048]{2,1,0:T(8,128)(2,1)} %collective-permute-done.2), kind=kOutput, calls=%fused_computation.1 | convolution fusion | flops 536870912 | bytes 3670016 | tf_op jit(solution)/shard_map/iap,jbp->iajb/dot_general | solution.py:61
  113.2 0.3 reshape.236
  113.4 0.8 copy.35
  114.3 3.5 %all-to-all-start.3 = ((f32[8,1,128,1,128]{4,2,3,1,0:T(8,128)}), f32[8,1,128,1,128]{4,2,3,1,0:T(8,128)S(1)}, u32[]{:S(2)}, u32[]{:S(2)}) async-start(f32[8,1,128,1,128]{4,2,3,1,0:T(8,128)} %bitcast.30), calls=%async_computation.3 | async-start | bytes 1048576 | tf_op jit(solution)/shard_map/all_to_all | solution.py:68
  117.8 0.0 reduce-scatter.2.cloned.1.call-start
  117.8 4.0 %fusion.10 = f32[512,2048]{1,0:T(8,128)} fusion(bf16[1,256,2048]{2,1,0:T(8,128)(2,1)} %collective-permute-done.1, f32[64,8,2,128]{3,2,1,0:T(2,128)S(1)} %bitcast.110, f32[512,256]{1,0:T(8,128)S(1)} %fusion.2, f32[512]{0:T(512)S(1)} %get-tuple-element.11, f32[256]{0:T(256)S(1)} %select_reduce_fusion.1), kind=kOutput, calls=%fused_computation.13 | convolution fusion | flops 537526272 | bytes 6294528 | tf_op jit(solution)/shard_map/iajb,jbp->iap/dot_general | solution.py:82
  121.8 0.3 copy.31
  122.0 4.0 %fusion.13 = f32[512,2048]{1,0:T(8,128)} fusion(bf16[1,256,2048]{2,1,0:T(8,128)(2,1)} %copy-done, f32[64,8,2,128]{3,2,1,0:T(2,128)S(1)} %bitcast.113, f32[512,256]{1,0:T(8,128)S(1)} %fusion.4, f32[512]{0:T(512)S(1)} %get-tuple-element.12, f32[256]{0:T(256)S(1)} %select_reduce_fusion.1), kind=kOutput, calls=%fused_computation.16 | convolution fusion | flops 537526272 | bytes 6294528 | tf_op jit(solution)/shard_map/iajb,jbp->iap/dot_general | solution.py:82
  126.0 0.5 all-to-all-done.3
  126.5 0.3 copy.37
  126.8 7.8 %add_bitcast_fusion = f32[1,512,2048]{2,1,0:T(8,128)} fusion(f32[512,2048]{1,0:T(8,128)} %fusion.10, f32[512,2048]{1,0:T(8,128)} %fusion.24, f32[512,2048]{1,0:T(8,128)} %fusion.13, bf16[1,256,2048]{2,1,0:T(8,128)(2,1)} %collective-permute-done.2, f32[64,8,2,128]{3,2,1,0:T(2,128)S(1)} %bitcast.112, f32[512,256]{1,0:T(8,128)S(1)} %fusion, ...), kind=kOutput, calls=%fused_computation | convolution fusion | flops 540672000 | bytes 18877440 | tf_op jit(solution)/shard_map/iajb,jbp->iap/dot_general | solution.py:82
  134.6 0.0 reduce-scatter.2.cloned.1.call-update
  134.6 45.5 %reduce-scatter.2.cloned.1.call-done = f32[1,128,2048]{2,1,0:T(8,128)} async-done(((f32[1,512,2048]{2,1,0:T(8,128)}), f32[1,128,2048]{2,1,0:T(8,128)}) %reduce-scatter.2.cloned.1.call-update) | async-done | bytes 1048592 | tf_op jit(solution)/shard_map/reduce_scatter | solution.py:85
  (7 shorter events, 0.0 us)
Async XLA Ops:
  6.5 26.4 %all-gather.6.cloned.1.call-start = ((), (), s32[]{:S(2)}) async-start(), calls=%async_computation.7 | async-start | bytes 1572864 | tf_op jit(solution)/shard_map/all_gather | solution.py:10
  7.3 65.8 %all-gather.4.cloned.1.call-start = ((), (), s32[]{:S(2)}) async-start(), calls=%async_computation.5 | async-start | bytes 2621440 | tf_op jit(solution)/shard_map/all_gather | solution.py:54
  32.9 26.7 %collective-permute-start = (bf16[1,256,2048]{2,1,0:T(8,128)(2,1)}, bf16[1,256,2048]{2,1,0:T(8,128)(2,1)S(1)}, u32[]{:S(2)}, u32[]{:S(2)}) collective-permute-start(bf16[1,256,2048]{2,1,0:T(8,128)(2,1)} %bitcast.119), channel_id=1, source_target_pairs={{24,0},{0,8},{8,16},{16,24},{25,1},{1,9},{9,17},{17,25},{26,2},{2,... | collective-permute-start | bytes 3145736 | tf_op jit(solution)/shard_map/ppermute | solution.py:18
  59.7 16.1 %copy-start = (bf16[1,256,2048]{2,1,0:T(8,128)(2,1)}, bf16[1,256,2048]{2,1,0:T(8,128)(2,1)S(1)}, u32[]{:S(2)}) copy-start(bf16[1,256,2048]{2,1,0:T(8,128)(2,1)S(1)} %collective-permute-done) | copy-start | bytes 3145732
  59.7 25.8 %collective-permute-start.1 = (bf16[1,256,2048]{2,1,0:T(8,128)(2,1)S(1)}, bf16[1,256,2048]{2,1,0:T(8,128)(2,1)}, u32[]{:S(2)}, u32[]{:S(2)}) collective-permute-start(bf16[1,256,2048]{2,1,0:T(8,128)(2,1)S(1)} %collective-permute-done), channel_id=1, source_target_pairs={{24,0},{0,8},{8,16},{16,24},{25,1},{1,9},{9,17},{17,25},{26,2},{2,... | collective-permute-start | bytes 3145736 | tf_op jit(solution)/shard_map/ppermute | solution.py:18
  76.9 12.3 %all-to-all-start = ((f32[8,1,128,1,128]{4,2,3,1,0:T(8,128)}), f32[8,1,128,1,128]{4,2,3,1,0:T(8,128)S(1)}, u32[]{:S(2)}, u32[]{:S(2)}) async-start(f32[8,1,128,1,128]{4,2,3,1,0:T(8,128)} %bitcast.4), calls=%async_computation | async-start | bytes 1048576 | tf_op jit(solution)/shard_map/all_to_all | solution.py:68
  85.4 25.1 %collective-permute-start.2 = (bf16[1,256,2048]{2,1,0:T(8,128)(2,1)}, bf16[1,256,2048]{2,1,0:T(8,128)(2,1)}, u32[]{:S(2)}, u32[]{:S(2)}) collective-permute-start(bf16[1,256,2048]{2,1,0:T(8,128)(2,1)} %collective-permute-done.1), channel_id=1, source_target_pairs={{24,0},{0,8},{8,16},{16,24},{25,1},{1,9},{9,17},{17,25},{26,2},{2,... | collective-permute-start | bytes 3145736 | tf_op jit(solution)/shard_map/ppermute | solution.py:18
  88.0 4.7 %copy-start.1 = (f32[1024]{0:T(1024)S(1)}, f32[1024]{0:T(1024)}, u32[]{:S(2)}) copy-start(f32[1024]{0:T(1024)} %param.7) | copy-start | bytes 12292
  89.2 12.3 %all-to-all-start.2 = ((f32[8,1,128,1,128]{4,2,3,1,0:T(8,128)}), f32[8,1,128,1,128]{4,2,3,1,0:T(8,128)S(1)}, u32[]{:S(2)}, u32[]{:S(2)}) async-start(f32[8,1,128,1,128]{4,2,3,1,0:T(8,128)} %bitcast.23), calls=%async_computation.2 | async-start | bytes 1048576 | tf_op jit(solution)/shard_map/all_to_all | solution.py:68
  101.5 12.8 %all-to-all-start.1 = ((f32[8,1,128,1,128]{4,2,3,1,0:T(8,128)}), f32[8,1,128,1,128]{4,2,3,1,0:T(8,128)S(1)}, u32[]{:S(2)}, u32[]{:S(2)}) async-start(f32[8,1,128,1,128]{4,2,3,1,0:T(8,128)} %bitcast.117), calls=%async_computation.1 | async-start | bytes 1048576 | tf_op jit(solution)/shard_map/all_to_all | solution.py:68
  114.3 12.3 %all-to-all-start.3 = ((f32[8,1,128,1,128]{4,2,3,1,0:T(8,128)}), f32[8,1,128,1,128]{4,2,3,1,0:T(8,128)S(1)}, u32[]{:S(2)}, u32[]{:S(2)}) async-start(f32[8,1,128,1,128]{4,2,3,1,0:T(8,128)} %bitcast.30), calls=%async_computation.3 | async-start | bytes 1048576 | tf_op jit(solution)/shard_map/all_to_all | solution.py:68
  117.8 62.4 %reduce-scatter.2.cloned.1.call-start = ((), (), s32[]{:S(2)}) async-start(), calls=%async_computation.6 | async-start | bytes 5242880 | tf_op jit(solution)/shard_map/reduce_scatter | solution.py:85
Sparse Core Ops, SparseCore 0:
  8.9 23.9 all-gather.5
  34.5 22.5 all-gather.3
  134.7 45.3 reduce-scatter.1
